TPU v7x, 32 devices: a whole 2x2x4 slice. The times are simulated.
32 devices in a mesh: frame: 2 (over y), orient: 4 (over x, core), pix: 4 (over z).
Axes of the slice: x: 2, y: 2, z: 4, core: 2. Of those that a mesh axis runs over, the one named last changes fastest.
Arguments:
- photon_counts: int32 [32, 16384], P('frame', 'pix'), may hold values from 0 to 8, as said below
- slices: bfloat16 [768, 16384], P('orient', 'pix'), may hold values from 0.049804688 to 2
- owner_ids: int32 [768, 128], P('orient', 'pix'), may hold values from 0 to 3
- tile_ids: int32 [768, 128], P('orient', 'pix'), may hold values from 0 to 2047
- patch_count: int32 [768], P('orient'), may hold values from 16 to 128
- old_model: float32 [1024, 128], P(('frame', 'orient', 'pix')), may hold values from 0.1 to 2
Outputs:
- orient_prob: bfloat16 [32, 768], P('frame', 'orient')
- merged: float32 [1024, 128], P(('frame', 'orient', 'pix'))
Inputs may be any that keep to these rules, and one draw needn't show every extreme that they name: `photon_counts`: each frame's counts stay below a level of 3 to 9 drawn for that frame.
All inputs are finite; a program needn't handle non-finite values.
Results may differ from a plain program's by a relative error of at most 0.0029.
The roundings to bfloat16 on the way count: a program that leaves them out, or rounds other values in their place, can miss the bound.
Values sent between devices are 32-bit elements; how exact they have to be, the bound alone decides.
No kernel may reach another device: no remote copies, remote signals or barrier semaphores. Data moves between devices by JAX's collectives and lax.ppermute only.
A program may use at most 64 MiB of HBM per device.

v0:
```python
import math

import jax
import jax.numpy as jnp
from jax import lax
from jax.sharding import PartitionSpec as P

P_SIZE = 16384
NB = 4
BRICK_ROWS = 256
SHIFTS = 8


def joined(part, axis, combine):
    gathered = jax.tree.map(lambda a: lax.all_gather(a, axis), part)

    def take(source):
        return jax.tree.map(lambda a: lax.dynamic_index_in_dim(a, source, 0, False), gathered)

    return lax.fori_loop(
        1, lax.axis_size(axis), lambda source, state: combine(state, take(source)), take(0)
    )


def deposit(values, weights, owners, tile_ids, live_mask, rows_total):
    shift_ids = tile_ids % SHIFTS
    inner_rows = tile_ids // SHIFTS
    moved = jnp.zeros(values.shape, jnp.float32)
    for shift in range(SHIFTS):
        rolled = jnp.roll(values, 17 * shift, axis=2)
        moved = jnp.where((shift_ids == shift)[:, :, None], rolled, moved)
    flat_values = (moved * live_mask[:, :, None]).reshape(-1, 128)
    flat_weights = (live_mask * weights[:, None]).reshape(-1, 1)
    flat_owners = owners.reshape(-1)
    flat_inner = inner_rows.reshape(-1)
    brick_lines = lax.iota(jnp.int32, BRICK_ROWS)

    def one_brick(brick):
        picked = (flat_inner[None, :] == brick_lines[:, None]) & (flat_owners[None, :] == brick)
        onehot = picked.astype(jnp.float32)
        summed = jnp.dot(
            onehot, flat_values, precision=lax.Precision.HIGHEST, preferred_element_type=jnp.float32
        )
        weighed = jnp.dot(
            onehot,
            flat_weights,
            precision=lax.Precision.HIGHEST,
            preferred_element_type=jnp.float32,
        )
        return (summed, weighed[:, 0])

    brick_sum, brick_weight = lax.map(one_brick, lax.iota(jnp.int32, rows_total // BRICK_ROWS))
    return (brick_sum.reshape(rows_total, 128), brick_weight.reshape(rows_total))


def combine_stats(earlier, latter):
    score_top = jnp.maximum(earlier[0], latter[0])
    summed = earlier[1] * jnp.exp(earlier[0] - score_top) + latter[1] * jnp.exp(
        latter[0] - score_top
    )
    return (score_top, summed)


def shards(photon_counts, slices, owner_ids, tile_ids, patch_count, old_model):
    orient_rows = slices.shape[0]
    pixel_cols = slices.shape[1]
    local_patches = pixel_cols // 128
    rows_total = NB * BRICK_ROWS
    frames_bf = photon_counts.astype(jnp.bfloat16)
    log_slice = jnp.log(slices.astype(jnp.float32)).astype(jnp.bfloat16)
    fit_part = jnp.einsum("fp,rp->fr", frames_bf, log_slice, preferred_element_type=jnp.float32)
    mass_part = jnp.sum(slices, axis=1, dtype=jnp.float32)
    fit, slice_mass = lax.psum((fit_part, mass_part), "pix")
    score = (fit - slice_mass[None, :]) * (1.0 / math.sqrt(P_SIZE))
    local_top = jnp.max(score, axis=1)
    local_total = jnp.sum(jnp.exp(score - local_top[:, None]), axis=1)
    score_top, score_total = joined((local_top, local_total), "orient", combine_stats)
    weights_exp = jnp.exp(score - score_top[:, None])
    orient_prob = (weights_exp / score_total[:, None]).astype(jnp.bfloat16)
    weight_part = jnp.sum(orient_prob.astype(jnp.float32), axis=0)
    photon_part = jnp.einsum(
        "fr,fp->rp", orient_prob, frames_bf, preferred_element_type=jnp.float32
    )
    pix_start = lax.axis_index("pix") * local_patches
    frame_count = lax.axis_size("frame")
    weight_tile = jnp.broadcast_to(weight_part[:, None], (orient_rows, frame_count))
    photon_sum, weight_sum = (
        lax.psum_scatter(photon_part, "frame", scatter_dimension=1, tiled=True),
        lax.psum_scatter(weight_tile, "frame", scatter_dimension=1, tiled=True),
    )
    held_patches = photon_sum.shape[1] // 128
    frame_start = lax.axis_index("frame") * held_patches
    owner_part = lax.dynamic_slice_in_dim(owner_ids, frame_start, held_patches, 1)
    tile_part = lax.dynamic_slice_in_dim(tile_ids, frame_start, held_patches, 1)
    patch_id = pix_start + frame_start + lax.iota(jnp.int32, held_patches)
    live_mask = (patch_id[None, :] < patch_count[:, None]).astype(jnp.float32)
    brick_part, weight_rows = deposit(
        photon_sum.reshape(orient_rows, held_patches, 128),
        weight_sum[:, 0],
        owner_part,
        tile_part,
        live_mask,
        rows_total,
    )
    brick_sum, brick_weight = (
        lax.psum_scatter(brick_part, ("frame", "orient", "pix"), scatter_dimension=0, tiled=True),
        lax.psum_scatter(weight_rows, ("frame", "orient", "pix"), scatter_dimension=0, tiled=True),
    )
    frames_total = photon_counts.shape[0] * lax.axis_size("frame")
    patches_total = pixel_cols * lax.axis_size("pix") // 128
    prior = frames_total * patches_total / (4.0 * rows_total)
    merged = (brick_sum + prior * old_model) / (brick_weight[:, None] + prior)
    return (orient_prob, merged)


def solution(mesh):
    placed = (
        P("frame", "pix"),
        P("orient", "pix"),
        P("orient", "pix"),
        P("orient", "pix"),
        P("orient"),
        P(("frame", "orient", "pix"), None),
    )
    return jax.shard_map(
        shards,
        mesh=mesh,
        in_specs=placed,
        out_specs=(P("frame", "orient"), P(("frame", "orient", "pix"), None)),
        check_vma=False,
    )
```

profile of v0, /device:TPU:0, one launch (start us, length us, event | category | flops | bytes accessed | tf_op | source)
XLA Modules:
  0.0 276.8 jit_solution(9964418669638546789)
XLA Ops:
  7.3 1.8 convert_reduce_fusion
  9.1 1.5 fusion.22
  10.6 20.7 %all-reduce.4 = (f32[16,192]{1,0:T(8,128)S(1)}, f32[192]{0:T(256)S(1)}) all-reduce(f32[16,192]{1,0:T(8,128)S(1)} %fusion.22, f32[192]{0:T(256)S(1)} %convert_reduce_fusion), channel_id=1, replica_groups=mesh['frame'=2,'orient'=4,'pix'=4] {'pix'}, use_global_device_ids=true, to_apply=%region_0.0 | all-reduce | flops 3264 | bytes 26112 | tf_op jit(solution)/shard_map/psum | solution.py:73
  31.3 0.1 fusion.30
  31.4 0.2 exponential_reduce_fusion
  31.6 0.6 dynamic-slice
  32.8 0.2 dynamic-update-slice
  33.1 0.2 dynamic-update-slice.1
  33.3 5.6 %all-reduce.5 = (f32[64]{0:T(128)S(1)}, f32[64]{0:T(128)S(1)}) all-reduce(f32[64]{0:T(128)S(1)} %dynamic-update-slice, f32[64]{0:T(128)S(1)} %dynamic-update-slice.1), channel_id=2, replica_groups=mesh['frame'=2,'orient'=4,'pix'=4] {'orient'}, use_global_device_ids=true, to_apply=%add | all-reduce | flops 128 | bytes 1024
  39.1 0.1 while.31
  39.3 2.3 fusion.26
  42.0 0.1 broadcast_in_dim.103
  42.1 0.1 broadcast_in_dim.105
  42.2 0.1 broadcast_in_dim.107
  42.3 0.1 broadcast_in_dim.109
  42.4 0.1 broadcast_in_dim.111
  42.6 0.1 broadcast_in_dim.113
  42.7 0.1 broadcast_in_dim.115
  42.8 0.1 broadcast_in_dim.101
  43.5 0.6 dynamic-slice.2
  44.1 4.9 %all-reduce.2 = f32[192,2]{0,1:T(2,128)S(1)} all-reduce(f32[192,2]{0,1:T(2,128)S(1)} %broadcast_in_dim.118), channel_id=5, replica_groups=mesh['frame'=2,'orient'=4,'pix'=4] {'frame'}, use_global_device_ids=true, to_apply=%region_9.10.clone | all-reduce | flops 384 | bytes 3072
  49.0 0.5 constant_dynamic-slice_fusion.1
  49.6 34.1 %reduce-scatter.3.cloned.1.call-done = f32[192,2048]{1,0:T(8,128)} async-done(((f32[192,4096]{1,0:T(8,128)}), f32[192,2048]{1,0:T(8,128)}) %reduce-scatter.3.cloned.1.call-update) | async-done | bytes 1572880 | tf_op jit(solution)/shard_map/reduce_scatter | solution.py:88
  83.7 1.7 copy.14
  85.4 1.7 slice.82
  87.1 1.6 slice.84
  88.8 1.6 slice.86
  90.4 1.6 slice.74
  92.0 1.6 slice.76
  93.6 1.6 slice.78
  95.3 1.6 slice.80
  96.9 1.4 reshape.148
  98.2 10.4 %fusion.24 = f32[3072,128]{1,0:T(8,128)S(1)} fusion(f32[3072,9]{1,0:T(8,128)S(1)} %bitcast.75, f32[3072,119]{1,0:T(8,128)} %bitcast.86, f32[3072,26]{1,0:T(8,128)S(1)} %bitcast.76, f32[3072,102]{1,0:T(8,128)} %bitcast.87, f32[3072,43]{1,0:T(8,128)S(1)} %bitcast.77, f32[3072,85]{1,0:T(8,128)} %bitcast.88, f32[3072,60]{1,0:T(8,128)S(1)} %bitcast.78, ...), kind=kLoop, calls=%fused_computation.25 | loop fusion | flops 6291456 | bytes 14192640 | tf_op jit(solution)/shard_map/mul | solution.py:32
  108.7 23.4 %while.32 = (s32[]{:T(128)}, f32[4,256,128]{2,1,0:T(8,128)}, f32[4,256]{1,0:T(4,128)S(1)}, s32[192,16]{1,0:T(8,128)}, s32[4]{0:T(128)S(1)}, /*index=5*/s32[192,1...) while((s32[]{:T(128)}, f32[4,256,128]{2,1,0:T(8,128)}, ...), condition=%wide.wide.region_11.12_spmd.clone, body=%wide.wide.region_10.11_spmd.clone.sunk | while | flops 1220551680 | bytes 1810641 | solution.py:52
  108.7 0.7 dynamic_slice.55
  109.4 0.7 broadcast_compare_fusion.11
  110.1 0.1 eq.147
  110.2 0.1 compare_select_fusion.3
  110.3 0.1 reshape.175
  110.4 1.6 fusion.53
  112.1 2.5 fusion.52
  114.6 0.7 dynamic_slice.55
  115.2 0.7 broadcast_compare_fusion.11
  115.9 0.1 eq.147
  116.1 0.1 compare_select_fusion.3
  116.2 0.1 reshape.175
  116.3 1.6 fusion.53
  117.9 2.5 fusion.52
  120.4 0.7 dynamic_slice.55
  121.1 0.7 broadcast_compare_fusion.11
  121.8 0.1 eq.147
  121.9 0.1 compare_select_fusion.3
  122.1 1.6 fusion.53
  123.7 2.5 fusion.52
  126.2 0.7 dynamic_slice.55
  126.9 0.7 broadcast_compare_fusion.11
  127.6 0.1 eq.147
  127.7 0.1 compare_select_fusion.3
  127.8 0.1 reshape.175
  127.9 1.6 fusion.53
  129.6 2.5 fusion.52
  132.1 39.5 %all-reduce.3 = f32[1024]{0:T(1024)S(1)} all-reduce(f32[1024]{0:T(1024)S(1)} %bitcast.94), channel_id=7, replica_groups=mesh['frame'=2,'orient'=4,'pix'=4] {'frame','orient','pix'}, use_global_device_ids=true, to_apply=%region_13.14.clone | all-reduce | flops 1024 | bytes 8192
  171.6 96.9 %reduce-scatter.5.cloned.1.call-done = f32[32,128]{1,0:T(8,128)} async-done(((f32[1024,128]{1,0:T(8,128)}), f32[32,128]{1,0:T(8,128)}) %reduce-scatter.5.cloned.1.call-update) | async-done | bytes 16400 | tf_op jit(solution)/shard_map/reduce_scatter | solution.py:106
  268.5 1.4 add_divide_fusion
  (59 shorter events, 1.7 us)
Async XLA Ops:
  7.2 34.5 %copy-start = (s32[192,32]{0,1:T(8,128)S(1)}, s32[192,32]{0,1:T(8,128)}, u32[]{:S(2)}) copy-start(s32[192,32]{0,1:T(8,128)} %param.13) | copy-start | bytes 73732
  7.2 1.9 copy-start.1
  7.2 76.5 %reduce-scatter.3.cloned.1.call-start = ((), (), s32[]{:S(2)}) async-start(), calls=%async_computation.2 | async-start | bytes 4718592 | tf_op jit(solution)/shard_map/reduce_scatter | solution.py:88
  7.2 24.3 %copy-start.10 = (u32[32]{0:T(128)S(1)}, u32[32]{0:T(128)}, u32[]{:S(2)}) copy-start(u32[32]{0:T(128)} %constant.123) | copy-start | bytes 388
  7.3 32.1 %copy-start.3 = (s32[16,4096]{1,0:T(8,128)S(1)}, s32[16,4096]{1,0:T(8,128)}, u32[]{:S(2)}) copy-start(s32[16,4096]{1,0:T(8,128)} %param.10) | copy-start | bytes 786436
  39.3 2.3 copy-start.6
  41.6 1.5 copy-start.5
  41.6 1.8 copy-start.8
  41.6 1.9 copy-start.9
  41.6 226.9 %reduce-scatter.5.cloned.1.call-start = ((), (), s32[]{:S(2)}) async-start(), calls=%async_computation.3 | async-start | bytes 540672 | tf_op jit(solution)/shard_map/reduce_scatter | solution.py:106
  43.3 42.1 %copy-start.4 = (s32[192,16]{1,0:T(8,128)}, s32[192,16]{1,0:T(8,128)S(1)}, u32[]{:S(2)}) copy-start(s32[192,16]{1,0:T(8,128)S(1)} %add_select_fusion.1) | copy-start | bytes 36868
  95.2 1.6 copy-start.2
  108.7 159.8 %copy-start.7 = (f32[32,128]{1,0:T(8,128)S(1)}, f32[32,128]{1,0:T(8,128)}, u32[]{:S(2)}) copy-start(f32[32,128]{1,0:T(8,128)} %param.15) | copy-start | bytes 49156
Sparse Core Ops, SparseCore 0:
  41.7 41.9 reduce-scatter.2
  132.2 136.2 reduce-scatter.4
where the time goes:
time: 277 us
  waiting for transfers between devices  131 us (47%)
  blocking collectives  70.7 us (26%)
  local copies, waits for them, and re-layouts  22 us (8%)
  matrix products  20 us (7%)
  other arithmetic  17.7 us (6%)
  between operations  15.1 us (5%)
    reduce_scatter x1, waiting for transfers between devices, shards(): lax.psum_scatter(brick_part, ('frame', 'orient', 'pix'), scatter_dimensio...  96.9 us
    unnamed x3, blocking collectives  50 us
    reduce_scatter x1, waiting for transfers between devices, shards(): lax.psum_scatter(photon_part, 'frame', scatter_dimension=1, tiled=True)  34.1 us
    psum x1, blocking collectives, shards(): fit, slice_mass = lax.psum((fit_part, mass_part), 'pix')  20.7 us
    slice x7, local copies, waits for them, and re-layouts, deposit(): rolled = jnp.roll(values, 17 * shift, axis=2)  11.5 us
    mul x1, other arithmetic, deposit(): flat_values = (moved * live_mask[:, :, None]).reshape(-1, 128)  10.4 us
    dot_general x4, matrix products, one_brick(): jnp.dot(onehot, flat_values, precision=lax.Precision.HIGHEST, preferred_e...  10 us
    dot_general x4, matrix products, one_brick(): jnp.dot(onehot, flat_weights, precision=lax.Precision.HIGHEST, preferred_...  6.29 us
  transfers between devices with their start and end apart: 2, of which 2 were waited for; matrix products, arithmetic and copies ran while one was open for 1% of the time, Pallas kernels for 0%

commit v1 on v0

--- a/solution.py
+++ b/solution.py
@@ -1,14 +1,19 @@
+import functools
 import math
 
 import jax
 import jax.numpy as jnp
 from jax import lax
+from jax.experimental import pallas as pl
+from jax.experimental.pallas import tpu as pltpu
 from jax.sharding import PartitionSpec as P
 
 P_SIZE = 16384
 NB = 4
 BRICK_ROWS = 256
 SHIFTS = 8
+STEP = 17
+LANES = 128
 
 
 def joined(part, axis, combine):
@@ -27,9 +32,9 @@
     inner_rows = tile_ids // SHIFTS
     moved = jnp.zeros(values.shape, jnp.float32)
     for shift in range(SHIFTS):
-        rolled = jnp.roll(values, 17 * shift, axis=2)
+        rolled = jnp.roll(values, STEP * shift, axis=2)
         moved = jnp.where((shift_ids == shift)[:, :, None], rolled, moved)
-    flat_values = (moved * live_mask[:, :, None]).reshape(-1, 128)
+    flat_values = (moved * live_mask[:, :, None]).reshape(-1, LANES)
     flat_weights = (live_mask * weights[:, None]).reshape(-1, 1)
     flat_owners = owners.reshape(-1)
     flat_inner = inner_rows.reshape(-1)
@@ -50,7 +55,7 @@
         return (summed, weighed[:, 0])
 
     brick_sum, brick_weight = lax.map(one_brick, lax.iota(jnp.int32, rows_total // BRICK_ROWS))
-    return (brick_sum.reshape(rows_total, 128), brick_weight.reshape(rows_total))
+    return (brick_sum.reshape(rows_total, LANES), brick_weight.reshape(rows_total))
 
 
 def combine_stats(earlier, latter):
@@ -61,10 +66,10 @@
     return (score_top, summed)
 
 
-def shards(photon_counts, slices, owner_ids, tile_ids, patch_count, old_model):
+def general_shards(photon_counts, slices, owner_ids, tile_ids, patch_count, old_model):
     orient_rows = slices.shape[0]
     pixel_cols = slices.shape[1]
-    local_patches = pixel_cols // 128
+    local_patches = pixel_cols // LANES
     rows_total = NB * BRICK_ROWS
     frames_bf = photon_counts.astype(jnp.bfloat16)
     log_slice = jnp.log(slices.astype(jnp.float32)).astype(jnp.bfloat16)
@@ -88,14 +93,14 @@
         lax.psum_scatter(photon_part, "frame", scatter_dimension=1, tiled=True),
         lax.psum_scatter(weight_tile, "frame", scatter_dimension=1, tiled=True),
     )
-    held_patches = photon_sum.shape[1] // 128
+    held_patches = photon_sum.shape[1] // LANES
     frame_start = lax.axis_index("frame") * held_patches
     owner_part = lax.dynamic_slice_in_dim(owner_ids, frame_start, held_patches, 1)
     tile_part = lax.dynamic_slice_in_dim(tile_ids, frame_start, held_patches, 1)
     patch_id = pix_start + frame_start + lax.iota(jnp.int32, held_patches)
     live_mask = (patch_id[None, :] < patch_count[:, None]).astype(jnp.float32)
     brick_part, weight_rows = deposit(
-        photon_sum.reshape(orient_rows, held_patches, 128),
+        photon_sum.reshape(orient_rows, held_patches, LANES),
         weight_sum[:, 0],
         owner_part,
         tile_part,
@@ -106,10 +111,231 @@
         lax.psum_scatter(brick_part, ("frame", "orient", "pix"), scatter_dimension=0, tiled=True),
         lax.psum_scatter(weight_rows, ("frame", "orient", "pix"), scatter_dimension=0, tiled=True),
     )
+    prior = prior_of(photon_counts, slices, rows_total)
+    merged = (brick_sum + prior * old_model) / (brick_weight[:, None] + prior)
+    return (orient_prob, merged)
+
+
+def prior_of(photon_counts, slices, rows_total):
     frames_total = photon_counts.shape[0] * lax.axis_size("frame")
-    patches_total = pixel_cols * lax.axis_size("pix") // 128
-    prior = frames_total * patches_total / (4.0 * rows_total)
-    merged = (brick_sum + prior * old_model) / (brick_weight[:, None] + prior)
+    patches_total = slices.shape[1] * lax.axis_size("pix") // LANES
+    return frames_total * patches_total / (4.0 * rows_total)
+
+
+def across(value, axis, mask):
+    count = lax.axis_size(axis)
+    return lax.ppermute(value, axis, [(i, i ^ mask) for i in range(count)])
+
+
+def across_two(value, axes, masks):
+    first, second = (lax.axis_size(axis) for axis in axes)
+    pairs = [
+        (i * second + j, (i ^ masks[0]) * second + (j ^ masks[1]))
+        for i in range(first)
+        for j in range(second)
+    ]
+    return lax.ppermute(value, axes, pairs)
+
+
+def fit_kernel(counts_ref, slices_ref, out_ref, mass_acc, fit_acc):
+    step = pl.program_id(0)
+
+    @pl.when(step == 0)
+    def _():
+        mass_acc[...] = jnp.zeros_like(mass_acc)
+        fit_acc[...] = jnp.zeros_like(fit_acc)
+
+    wide = slices_ref[...].astype(jnp.float32)
+    total = wide[:, :LANES]
+    for start in range(LANES, wide.shape[1], LANES):
+        total = total + wide[:, start : start + LANES]
+    mass_acc[...] += total
+    log_slice = jnp.log(wide).astype(jnp.bfloat16)
+    frames_bf = counts_ref[...].astype(jnp.float32).astype(jnp.bfloat16)
+    fit_acc[...] += lax.dot_general(
+        frames_bf, log_slice, (((1,), (1,)), ((), ())), preferred_element_type=jnp.float32
+    )
+
+    @pl.when(step == pl.num_programs(0) - 1)
+    def _():
+        ones = jnp.ones((out_ref.shape[0], LANES), jnp.float32)
+        mass = lax.dot_general(
+            ones,
+            mass_acc[...],
+            (((1,), (1,)), ((), ())),
+            precision=lax.Precision.HIGHEST,
+            preferred_element_type=jnp.float32,
+        )
+        out_ref[...] = fit_acc[...] - mass
+
+
+def fit_less_mass(photon_counts, slices):
+    frames, pixels = photon_counts.shape
+    orients = slices.shape[0]
+    chunk = math.gcd(pixels, 1024)
+    return pl.pallas_call(
+        fit_kernel,
+        grid=(pixels // chunk,),
+        in_specs=[
+            pl.BlockSpec((frames, chunk), lambda i: (0, i)),
+            pl.BlockSpec((orients, chunk), lambda i: (0, i)),
+        ],
+        out_specs=pl.BlockSpec((frames, orients), lambda i: (0, 0)),
+        out_shape=jax.ShapeDtypeStruct((frames, orients), jnp.float32),
+        scratch_shapes=[
+            pltpu.VMEM((orients, LANES), jnp.float32),
+            pltpu.VMEM((frames, orients), jnp.float32),
+        ],
+        name="fit",
+    )(photon_counts, slices)
+
+
+def rolled_kernel(groups, *refs):
+    count_refs, out_ref = refs[:-1], refs[-1]
+    rows = count_refs[0].shape[0]
+    for group, count_ref in enumerate(count_refs):
+        for patch in range(out_ref.shape[0]):
+            part = count_ref[:, patch * LANES : (patch + 1) * LANES].astype(jnp.float32)
+            for shift in range(SHIFTS):
+                turned = pltpu.roll(part, (STEP * shift) % LANES, 1) if shift else part
+                at = (shift * groups + group) * rows
+                out_ref[patch, at : at + rows, :] = turned.astype(jnp.bfloat16)
+
+
+def rolled_frames(counts):
+    frames, pixels = counts[0].shape
+    patches = pixels // LANES
+    block = math.gcd(patches, 4)
+    return pl.pallas_call(
+        functools.partial(rolled_kernel, len(counts)),
+        grid=(patches // block,),
+        in_specs=[pl.BlockSpec((frames, block * LANES), lambda i: (0, i)) for _ in counts],
+        out_specs=pl.BlockSpec((block, SHIFTS * len(counts) * frames, LANES), lambda i: (i, 0, 0)),
+        out_shape=jax.ShapeDtypeStruct(
+            (patches, SHIFTS * len(counts) * frames, LANES), jnp.bfloat16
+        ),
+        name="rolled",
+    )(*counts)
+
+
+def deposit_kernel(groups, orients, scale, where_ref, *refs):
+    score_refs = refs[: groups * orients]
+    id_refs = refs[groups * orients : groups * orients + orients]
+    rolled_ref = refs[groups * orients + orients]
+    prob_ref = refs[groups * orients + orients + 1]
+    piece_refs = refs[groups * orients + orients + 2 : -4]
+    ids, probs, summed, weighed = refs[-4:]
+    frames, width = score_refs[0].shape
+    patches = rolled_ref.shape[0]
+    rows = summed.shape[0]
+    columns = orients * width
+
+    for group in range(groups):
+        scores = [score_refs[group * orients + b][...] * scale for b in range(orients)]
+        top = functools.reduce(jnp.maximum, [jnp.max(s, axis=1, keepdims=True) for s in scores])
+        parts = [jnp.exp(s - top) for s in scores]
+        total = functools.reduce(jnp.add, [jnp.sum(s, axis=1, keepdims=True) for s in parts])
+        for b in range(orients):
+            prob = (parts[b] / total).astype(jnp.bfloat16)
+            if group == 0 and b == 0:
+                prob_ref[...] = prob
+            probs[group * frames : (group + 1) * frames, b * width : (b + 1) * width] = prob.astype(
+                jnp.float32
+            )
+    for b in range(orients):
+        ids[:, b * width : (b + 1) * width] = id_refs[b][...]
+
+    base = where_ref[0]
+    lines = lax.broadcasted_iota(jnp.int32, (rows, columns), 0) + base
+    summed[...] = jnp.zeros_like(summed)
+    weighed[...] = jnp.zeros_like(weighed)
+
+    def one_patch(patch, carry):
+        row = ids[pl.ds(patch, 1), :]
+        shift_of = ids[pl.ds(patches + patch, 1), :]
+        onehot = jnp.where(row == lines, 1.0, 0.0).astype(jnp.bfloat16)
+        prob = probs[...]
+        masked = jnp.concatenate(
+            [
+                jnp.where(shift_of == shift, prob, 0.0).astype(jnp.bfloat16)
+                for shift in range(SHIFTS)
+            ],
+            axis=0,
+        )
+        picked = lax.dot_general(
+            onehot, masked, (((1,), (1,)), ((), ())), preferred_element_type=jnp.float32
+        )
+        weighed[...] += picked
+        summed[...] += jnp.dot(
+            picked.astype(jnp.bfloat16), rolled_ref[patch], preferred_element_type=jnp.float32
+        )
+        return carry
+
+    lax.fori_loop(0, patches, one_patch, 0)
+
+    heavy = jnp.broadcast_to(jnp.sum(weighed[...], axis=1, keepdims=True), (rows, LANES))
+    weighed[:, :LANES] = heavy
+    held = piece_refs[0].shape[0] // 2
+    for k, piece in enumerate(piece_refs):
+        start = pl.multiple_of((where_ref[1] ^ k) * held, held)
+        piece[:held, :] = summed[pl.ds(start, held), :]
+        piece[held:, :] = weighed[pl.ds(start, held), :LANES]
+
+
+def deposited(where, scores, ids, rolled, groups, scale, rows, pieces):
+    frames, width = scores[0].shape
+    orients = len(ids)
+    held = rows // pieces
+    in_vmem = pl.BlockSpec(memory_space=pltpu.VMEM)
+    columns = orients * width
+    return pl.pallas_call(
+        functools.partial(deposit_kernel, groups, orients, scale),
+        in_specs=[pl.BlockSpec(memory_space=pltpu.SMEM)]
+        + [in_vmem] * (len(scores) + len(ids) + 1),
+        out_specs=[in_vmem] * (1 + pieces),
+        out_shape=[jax.ShapeDtypeStruct((frames, width), jnp.bfloat16)]
+        + [jax.ShapeDtypeStruct((2 * held, LANES), jnp.float32)] * pieces,
+        scratch_shapes=[
+            pltpu.VMEM((ids[0].shape[0], columns), jnp.int32),
+            pltpu.VMEM((groups * frames, columns), jnp.float32),
+            pltpu.VMEM((rows, LANES), jnp.float32),
+            pltpu.VMEM((rows, rolled.shape[1]), jnp.float32),
+        ],
+        name="deposit",
+    )(where, *scores, *ids, rolled)
+
+
+def direct_shards(photon_counts, slices, owner_ids, tile_ids, patch_count, old_model):
+    rows_total = NB * BRICK_ROWS
+    local_patches = slices.shape[1] // LANES
+    groups, orients, pieces = (lax.axis_size(axis) for axis in ("frame", "orient", "pix"))
+    rows = rows_total // (groups * orients)
+    pix_at = lax.axis_index("pix")
+
+    counts = [photon_counts] + [across(photon_counts, "frame", g) for g in range(1, groups)]
+    patch_id = pix_at * local_patches + lax.iota(jnp.int32, local_patches)
+    row_index = owner_ids * BRICK_ROWS + tile_ids // SHIFTS
+    row_index = jnp.where(patch_id[None, :] < patch_count[:, None], row_index, -1)
+    own_ids = jnp.concatenate([row_index.T, (tile_ids % SHIFTS).T], axis=0)
+    ids = [own_ids] + [across(own_ids, "orient", b) for b in range(1, orients)]
+    rolled = rolled_frames(counts)
+
+    part = fit_less_mass(photon_counts, slices)
+    score = part + functools.reduce(jnp.add, [across(part, "pix", k) for k in range(1, pieces)])
+    scores = [
+        score if not (g or b) else across_two(score, ("frame", "orient"), (g, b))
+        for g in range(groups)
+        for b in range(orients)
+    ]
+    base = (lax.axis_index("frame") * orients + lax.axis_index("orient")) * rows
+    where = jnp.stack([base, pix_at]).astype(jnp.int32)
+    orient_prob, *own = deposited(
+        where, scores, ids, rolled, groups, 1.0 / math.sqrt(P_SIZE), rows, pieces
+    )
+    total = own[0] + functools.reduce(jnp.add, [across(own[k], "pix", k) for k in range(1, pieces)])
+    held = rows // pieces
+    prior = prior_of(photon_counts, slices, rows_total)
+    merged = (total[:held] + prior * old_model) / (total[held:] + prior)
     return (orient_prob, merged)
 
 
@@ -122,8 +348,11 @@
         P("orient"),
         P(("frame", "orient", "pix"), None),
     )
+    small = mesh.shape["frame"] <= 2 and all(
+        mesh.shape[axis] in (1, 2, 4) for axis in ("orient", "pix")
+    )
     return jax.shard_map(
-        shards,
+        direct_shards if small else general_shards,
         mesh=mesh,
         in_specs=placed,
         out_specs=(P("frame", "orient"), P(("frame", "orient", "pix"), None)),

time: 277 us -> 59.3 us (0.21)
  waiting for transfers between devices: 131 us -> 6.2 us
  blocking collectives: 70.7 us -> 0 us
  Pallas kernels: 0 us -> 25.5 us
  starting transfers between devices: 0.08 us -> 21.1 us
  local copies, waits for them, and re-layouts: 22 us -> 1.22 us
  matrix products: 20 us -> 0 us
  between operations: 15.1 us -> 0.82 us
  other arithmetic: 17.7 us -> 3.52 us
    reduce_scatter x2 -> x0, waiting for transfers between devices: 131 us -> none  [the longest x1 96.9 us: shards(): lax.psum_scatter(brick_part, ('frame', 'orient', 'pix'), scatter_dimensio...]
    unnamed x3 -> x0, blocking collectives: 50 us -> none
    pallas_call x0 -> x3, Pallas kernels: none -> 25.5 us  [the longest x1 16.6 us: deposited(): pl.pallas_call(functools.partial(deposit_kernel, groups, orients, scale),...]
    ppermute x0 -> x17, starting transfers between devices: none -> 21.1 us  [the longest x10 14.4 us: across(): return lax.ppermute(value, axis, [(i, i ^ mask) for i in range(count)])]
    psum x1 -> x0, blocking collectives: 20.7 us -> none  [shards(): fit, slice_mass = lax.psum((fit_part, mass_part), 'pix')]
    dot_general x10 -> x0, matrix products: 20 us -> none  [the longest x4 10 us: one_brick(): jnp.dot(onehot, flat_values, precision=lax.Precision.HIGHEST, preferred_e...]
    slice x7 -> x0, local copies, waits for them, and re-layouts: 11.5 us -> none  [deposit(): rolled = jnp.roll(values, 17 * shift, axis=2)]
    mul x5 -> x0, other arithmetic: 10.9 us -> none  [the longest x1 10.4 us: deposit(): flat_values = (moved * live_mask[:, :, None]).reshape(-1, 128)]
  transfers between devices with their start and end apart: 2 -> 17, of which waited for: 2 -> 3; matrix products, arithmetic and copies ran while one was open for 1% -> 4% of each run, Pallas kernels for 0% -> 9%
where the time goes in v1:
time: 59.3 us; the launch traced here: 58.4 us
  Pallas kernels  25.5 us (43%)
  starting transfers between devices  21.1 us (36%)
  waiting for transfers between devices  6.2 us (10%)
  other arithmetic  3.52 us (6%)
  local copies, waits for them, and re-layouts  1.22 us (2%)
  between operations  0.82 us (1%)
    pallas_call x1, Pallas kernels, deposited(): pl.pallas_call(functools.partial(deposit_kernel, groups, orients, scale),...  16.6 us
    ppermute x10, starting transfers between devices, across(): return lax.ppermute(value, axis, [(i, i ^ mask) for i in range(count)])  14.4 us
    ppermute x7, starting transfers between devices, across_two(): return lax.ppermute(value, axes, pairs)  6.77 us
    ppermute x10, waiting for transfers between devices, across(): return lax.ppermute(value, axis, [(i, i ^ mask) for i in range(count)])  6.18 us
    pallas_call x1, Pallas kernels, rolled_frames(): pl.pallas_call(functools.partial(rolled_kernel, len(counts)), grid=(patch...  5.22 us
    pallas_call x1, Pallas kernels, fit_less_mass(): pl.pallas_call(fit_kernel, grid=(pixels // chunk,), in_specs=[pl.BlockSpe...  3.75 us
    unnamed x28, local copies, waits for them, and re-layouts  1.22 us
  transfers between devices with their start and end apart: 17, of which 3 were waited for; matrix products, arithmetic and copies ran while one was open for 4% of the time, Pallas kernels for 9%

profile of v1, /device:TPU:0, one launch (start us, length us, event | category | flops | bytes accessed | tf_op | source)
XLA Modules:
  0.0 58.4 jit_solution(15550311275938975902)
XLA Ops:
  0.6 3.8 %fit.1 = f32[16,192]{1,0:T(8,128)} custom-call(s32[16,4096]{1,0:T(8,128)} %refs_0_.1, bf16[192,4096]{1,0:T(8,128)(2,1)} %slices_ref.1), custom_call_target="tpu_custom_call" | custom-call | tf_op jit(solution)/shard_map/fit/pallas_call | solution.py:176
  4.4 5.1 %collective-permute-start.2 = (f32[16,192]{1,0:T(8,128)}, f32[16,192]{1,0:T(8,128)S(1)}, u32[]{:S(2)}, u32[]{:S(2)}) collective-permute-start(f32[16,192]{1,0:T(8,128)} %fit.1), channel_id=1, source_target_pairs={{0,3},{1,2},{2,1},{3,0},{4,7},{5,6},{6,5},{7,4},{8,11},{9,10},{10,... | collective-permute-start | bytes 36872 | tf_op jit(solution)/shard_map/ppermute | solution.py:127
  9.5 0.0 collective-permute-start.1
  9.5 0.6 collective-permute-start
  10.0 1.7 %collective-permute-start.13 = (s32[16,4096]{1,0:T(8,128)}, s32[16,4096]{1,0:T(8,128)S(1)}, u32[]{:S(2)}, u32[]{:S(2)}) collective-permute-start(s32[16,4096]{1,0:T(8,128)} %refs_0_.1), channel_id=1, source_target_pairs={{0,16},{16,0},{1,17},{17,1},{2,18},{18,2},{3,19},{19,3},{4,20},{20... | collective-permute-start | bytes 786440 | tf_op jit(solution)/shard_map/ppermute | solution.py:127
  11.8 0.0 collective-permute-done.2
  11.8 2.5 %collective-permute-done.1 = f32[16,192]{1,0:T(8,128)S(1)} collective-permute-done((f32[16,192]{1,0:T(8,128)}, f32[16,192]{1,0:T(8,128)S(1)}, u32[]{:S(2)}, u32[]{:S(2)}) %collective-permute-start.1) | collective-permute-done | bytes 12320 | tf_op jit(solution)/shard_map/ppermute | solution.py:127
  14.3 0.0 collective-permute-done
  14.3 0.7 %add_add_fusion.1.refs_0_ = f32[16,192]{1,0:T(8,128)S(1)} fusion(f32[16,192]{1,0:T(8,128)} %fit.1, f32[16,192]{1,0:T(8,128)S(1)} %collective-permute-done.2, f32[16,192]{1,0:T(8,128)S(1)} %collective-permute-done, f32[16,192]{1,0:T(8,128)S(1)} %collective-permute-done.1), kind=kLoop, calls=%fused_computation.17 | loop fusion | flops 9216 | bytes 61440 | tf_op jit(solution)/shard_map/add | solution.py:324
  15.0 0.0 copy-start.2
  15.0 0.5 collective-permute-start.9
  15.6 0.8 %fusion.2 = (s32[32,192]{1,0:T(8,128)S(1)}, s32[32,192]{1,0:T(8,128)S(1)}) fusion(s32[192,32]{0,1:T(8,128)} %param.8, s32[192,32]{0,1:T(8,128)} %param.9, s32[192]{0:T(256)} %param.10, s32[32]{0:T(128)S(1)} %iota_add_fusion), kind=kLoop, calls=%fused_computation.8 | loop fusion | flops 141312 | bytes 99200 | tf_op jit(solution)/shard_map/transpose | solution.py:319
  16.4 2.0 %collective-permute-start.8 = (f32[16,192]{1,0:T(8,128)S(1)}, f32[16,192]{1,0:T(8,128)S(1)}, u32[]{:S(2)}, u32[]{:S(2)}) collective-permute-start(f32[16,192]{1,0:T(8,128)S(1)} %add_add_fusion.1.refs_0_), channel_id=1, source_target_pairs={{0,24},{4,28},{8,16},{12,20},{16,8},{20,12},{24,0},{28,4},{1,25},{... | collective-permute-start | bytes 36872 | tf_op jit(solution)/shard_map/ppermute | solution.py:137
  18.4 1.4 %collective-permute-start.7 = (f32[16,192]{1,0:T(8,128)S(1)}, f32[16,192]{1,0:T(8,128)S(1)}, u32[]{:S(2)}, u32[]{:S(2)}) collective-permute-start(f32[16,192]{1,0:T(8,128)S(1)} %add_add_fusion.1.refs_0_), channel_id=1, source_target_pairs={{0,20},{4,16},{8,28},{12,24},{16,4},{20,0},{24,12},{28,8},{1,21},{... | collective-permute-start | bytes 36872 | tf_op jit(solution)/shard_map/ppermute | solution.py:137
  19.9 0.5 collective-permute-start.6
  20.4 0.0 collective-permute-done.9.refs_7_
  20.4 0.0 copy-start.6
  20.4 0.7 %collective-permute-start.5 = (f32[16,192]{1,0:T(8,128)S(1)}, f32[16,192]{1,0:T(8,128)S(1)}, u32[]{:S(2)}, u32[]{:S(2)}) collective-permute-start(f32[16,192]{1,0:T(8,128)S(1)} %add_add_fusion.1.refs_0_), channel_id=1, source_target_pairs={{0,12},{4,8},{8,4},{12,0},{16,28},{20,24},{24,20},{28,16},{1,13},{... | collective-permute-start | bytes 36872 | tf_op jit(solution)/shard_map/ppermute | solution.py:137
  21.1 0.0 copy-start.1
  21.1 0.0 collective-permute-done.8.refs_6_
  21.1 0.0 copy-start.7
  21.1 1.1 %collective-permute-start.12 = (s32[64,192]{1,0:T(8,128)S(1)}, s32[64,192]{1,0:T(8,128)S(1)}, u32[]{:S(2)}, u32[]{:S(2)}) collective-permute-start(s32[64,192]{1,0:T(8,128)S(1)} %pad_add_fusion.refs_8_), channel_id=1, source_target_pairs={{0,12},{4,8},{8,4},{12,0},{1,13},{5,9},{9,5},{13,1},{2,14},{6,10},... | collective-permute-start | bytes 147464 | tf_op jit(solution)/shard_map/ppermute | solution.py:127
  22.2 0.0 collective-permute-done.7.refs_5_
  22.2 1.5 %collective-permute-start.11 = (s32[64,192]{1,0:T(8,128)S(1)}, s32[64,192]{1,0:T(8,128)S(1)}, u32[]{:S(2)}, u32[]{:S(2)}) collective-permute-start(s32[64,192]{1,0:T(8,128)S(1)} %pad_add_fusion.refs_8_), channel_id=1, source_target_pairs={{0,8},{4,12},{8,0},{12,4},{1,9},{5,13},{9,1},{13,5},{2,10},{6,14},... | collective-permute-start | bytes 147464 | tf_op jit(solution)/shard_map/ppermute | solution.py:127
  23.7 0.0 collective-permute-done.6.refs_4_
  23.7 0.0 collective-permute-start.10
  23.7 0.0 collective-permute-done.5.refs_3_
  23.8 0.0 copy-start.10
  23.8 1.4 %collective-permute-start.4 = (f32[16,192]{1,0:T(8,128)S(1)}, f32[16,192]{1,0:T(8,128)S(1)}, u32[]{:S(2)}, u32[]{:S(2)}) collective-permute-start(f32[16,192]{1,0:T(8,128)S(1)} %add_add_fusion.1.refs_0_), channel_id=1, source_target_pairs={{0,8},{4,12},{8,0},{12,4},{16,24},{20,28},{24,16},{28,20},{1,9},{5... | collective-permute-start | bytes 36872 | tf_op jit(solution)/shard_map/ppermute | solution.py:137
  25.2 0.0 collective-permute-done.13.refs_1_
  25.2 0.2 collective-permute-start.3
  25.3 0.6 pad_add_fusion.1.where_ref
  25.9 0.0 copy-done
  25.9 5.2 %rolled.1.refs_12_ = bf16[32,256,128]{2,1,0:T(8,128)(2,1)} custom-call(s32[16,4096]{1,0:T(8,128)} %refs_0_.1, s32[16,4096]{1,0:T(8,128)} %copy-done), custom_call_target="tpu_custom_call" | custom-call | tf_op jit(solution)/shard_map/rolled/pallas_call | solution.py:209
  31.1 0.0 collective-permute-done.4.refs_2_
  31.1 0.0 collective-permute-done.3.refs_1_
  31.1 0.0 copy-start.12
  31.1 0.0 collective-permute-done.12.refs_11_
  31.2 0.0 copy-start.3
  31.2 0.0 collective-permute-done.11.refs_10_
  31.2 0.0 copy-start.4
  31.2 0.0 collective-permute-done.10.refs_9_
  31.2 0.0 copy-done.2
  31.2 0.0 copy-done.6
  31.2 0.0 copy-done.1
  31.2 0.0 copy-done.7
  31.2 0.0 copy-done.8
  31.2 0.0 copy-done.9
  31.3 0.0 copy-done.10
  31.3 0.5 copy-done.11
  31.7 0.0 copy-done.12
  31.7 0.0 copy-done.3
  31.8 0.0 copy-done.4
  31.8 0.6 %copy-done.5 = s32[64,192]{1,0:T(8,128)} copy-done((s32[64,192]{1,0:T(8,128)}, s32[64,192]{1,0:T(8,128)S(1)}, u32[]{:S(2)}) %copy-start.5) | copy-done | bytes 49176
  32.4 16.6 %deposit.1 = (bf16[16,192]{1,0:T(8,128)(2,1)}, f32[64,128]{1,0:T(8,128)}, f32[64,128]{1,0:T(8,128)}, f32[64,128]{1,0:T(8,128)}, f32[64,128]{1,0:T(8,128)}) custom-call(s32[2]{0:T(128)} %pad_add_fusion.1.where_ref, f32[16,192]{1,0:T(8,128)} %copy-done.2, f32[16,192]{1,0:T(8,128)} %copy-done.12, f32[16,192]{1,0:T(8,128)} %copy-done.11, f32[16,192]{1,0:T(8,128)} %copy-done.10, ...), custom_call_target="tpu_custom_call" | custom-call | tf_op jit(solution)/shard_map/deposit/pallas_call | solution.py:291
  49.0 0.0 collective-permute-start.14
  49.0 2.1 %collective-permute-start.15 = (f32[64,128]{1,0:T(8,128)}, f32[64,128]{1,0:T(8,128)S(1)}, u32[]{:S(2)}, u32[]{:S(2)}) collective-permute-start(f32[64,128]{1,0:T(8,128)} %get-tuple-element.10), channel_id=1, source_target_pairs={{0,2},{1,3},{2,0},{3,1},{4,6},{5,7},{6,4},{7,5},{8,10},{9,11},{10,... | collective-permute-start | bytes 98312 | tf_op jit(solution)/shard_map/ppermute | solution.py:127
  51.1 2.3 %collective-permute-start.16 = (f32[64,128]{1,0:T(8,128)}, f32[64,128]{1,0:T(8,128)S(1)}, u32[]{:S(2)}, u32[]{:S(2)}) collective-permute-start(f32[64,128]{1,0:T(8,128)} %get-tuple-element.11), channel_id=1, source_target_pairs={{0,3},{1,2},{2,1},{3,0},{4,7},{5,6},{6,5},{7,4},{8,11},{9,10},{10,... | collective-permute-start | bytes 98312 | tf_op jit(solution)/shard_map/ppermute | solution.py:127
  53.4 0.0 collective-permute-done.14
  53.4 0.7 %collective-permute-done.15 = f32[64,128]{1,0:T(8,128)S(1)} collective-permute-done((f32[64,128]{1,0:T(8,128)}, f32[64,128]{1,0:T(8,128)S(1)}, u32[]{:S(2)}, u32[]{:S(2)}) %collective-permute-start.15) | collective-permute-done | bytes 32800 | tf_op jit(solution)/shard_map/ppermute | solution.py:127
  54.1 2.9 %collective-permute-done.16 = f32[64,128]{1,0:T(8,128)S(1)} collective-permute-done((f32[64,128]{1,0:T(8,128)}, f32[64,128]{1,0:T(8,128)S(1)}, u32[]{:S(2)}, u32[]{:S(2)}) %collective-permute-start.16) | collective-permute-done | bytes 32800 | tf_op jit(solution)/shard_map/ppermute | solution.py:127
  57.0 0.8 %add_add_fusion = f32[64,128]{1,0:T(8,128)S(1)} fusion(f32[64,128]{1,0:T(8,128)} %get-tuple-element.8, f32[64,128]{1,0:T(8,128)S(1)} %collective-permute-done.16, f32[64,128]{1,0:T(8,128)S(1)} %collective-permute-done.14, f32[64,128]{1,0:T(8,128)S(1)} %collective-permute-done.15), kind=kLoop, calls=%fused_computation.10 | loop fusion | flops 24576 | bytes 163840 | tf_op jit(solution)/shard_map/add | solution.py:335
  57.8 0.0 copy-done.13
  57.8 0.6 %fusion.6 = f32[32,128]{1,0:T(8,128)} fusion(f32[64,128]{1,0:T(8,128)S(1)} %add_add_fusion, f32[32,128]{1,0:T(8,128)S(1)} %copy-done.13), kind=kLoop, calls=%fused_computation.15 | loop fusion | flops 12288 | bytes 65536 | tf_op jit(solution)/shard_map/div | solution.py:338
  (8 shorter events, 0.0 us)
Async XLA Ops:
  4.4 7.4 %collective-permute-start.2 = (f32[16,192]{1,0:T(8,128)}, f32[16,192]{1,0:T(8,128)S(1)}, u32[]{:S(2)}, u32[]{:S(2)}) collective-permute-start(f32[16,192]{1,0:T(8,128)} %fit.1), channel_id=1, source_target_pairs={{0,3},{1,2},{2,1},{3,0},{4,7},{5,6},{6,5},{7,4},{8,11},{9,10},{10,... | collective-permute-start | bytes 36872 | tf_op jit(solution)/shard_map/ppermute | solution.py:127
  9.5 4.8 %collective-permute-start.1 = (f32[16,192]{1,0:T(8,128)}, f32[16,192]{1,0:T(8,128)S(1)}, u32[]{:S(2)}, u32[]{:S(2)}) collective-permute-start(f32[16,192]{1,0:T(8,128)} %fit.1), channel_id=1, source_target_pairs={{0,2},{1,3},{2,0},{3,1},{4,6},{5,7},{6,4},{7,5},{8,10},{9,11},{10,... | collective-permute-start | bytes 36872 | tf_op jit(solution)/shard_map/ppermute | solution.py:127
  9.5 4.8 %collective-permute-start = (f32[16,192]{1,0:T(8,128)}, f32[16,192]{1,0:T(8,128)S(1)}, u32[]{:S(2)}, u32[]{:S(2)}) collective-permute-start(f32[16,192]{1,0:T(8,128)} %fit.1), channel_id=1, source_target_pairs={{0,1},{1,0},{2,3},{3,2},{4,5},{5,4},{6,7},{7,6},{8,9},{9,8},{10,11... | collective-permute-start | bytes 36872 | tf_op jit(solution)/shard_map/ppermute | solution.py:127
  10.0 15.2 %collective-permute-start.13 = (s32[16,4096]{1,0:T(8,128)}, s32[16,4096]{1,0:T(8,128)S(1)}, u32[]{:S(2)}, u32[]{:S(2)}) collective-permute-start(s32[16,4096]{1,0:T(8,128)} %refs_0_.1), channel_id=1, source_target_pairs={{0,16},{16,0},{1,17},{17,1},{2,18},{18,2},{3,19},{19,3},{4,20},{20... | collective-permute-start | bytes 786440 | tf_op jit(solution)/shard_map/ppermute | solution.py:127
  15.0 16.2 %copy-start.2 = (f32[16,192]{1,0:T(8,128)}, f32[16,192]{1,0:T(8,128)S(1)}, u32[]{:S(2)}) copy-start(f32[16,192]{1,0:T(8,128)S(1)} %add_add_fusion.1.refs_0_) | copy-start | bytes 36868
  15.0 5.3 %collective-permute-start.9 = (f32[16,192]{1,0:T(8,128)S(1)}, f32[16,192]{1,0:T(8,128)S(1)}, u32[]{:S(2)}, u32[]{:S(2)}) collective-permute-start(f32[16,192]{1,0:T(8,128)S(1)} %add_add_fusion.1.refs_0_), channel_id=1, source_target_pairs={{0,28},{4,24},{8,20},{12,16},{16,12},{20,8},{24,4},{28,0},{1,29},{... | collective-permute-start | bytes 36872 | tf_op jit(solution)/shard_map/ppermute | solution.py:137
  16.4 4.7 %collective-permute-start.8 = (f32[16,192]{1,0:T(8,128)S(1)}, f32[16,192]{1,0:T(8,128)S(1)}, u32[]{:S(2)}, u32[]{:S(2)}) collective-permute-start(f32[16,192]{1,0:T(8,128)S(1)} %add_add_fusion.1.refs_0_), channel_id=1, source_target_pairs={{0,24},{4,28},{8,16},{12,20},{16,8},{20,12},{24,0},{28,4},{1,25},{... | collective-permute-start | bytes 36872 | tf_op jit(solution)/shard_map/ppermute | solution.py:137
  18.4 3.8 %collective-permute-start.7 = (f32[16,192]{1,0:T(8,128)S(1)}, f32[16,192]{1,0:T(8,128)S(1)}, u32[]{:S(2)}, u32[]{:S(2)}) collective-permute-start(f32[16,192]{1,0:T(8,128)S(1)} %add_add_fusion.1.refs_0_), channel_id=1, source_target_pairs={{0,20},{4,16},{8,28},{12,24},{16,4},{20,0},{24,12},{28,8},{1,21},{... | collective-permute-start | bytes 36872 | tf_op jit(solution)/shard_map/ppermute | solution.py:137
  19.9 3.9 %collective-permute-start.6 = (f32[16,192]{1,0:T(8,128)S(1)}, f32[16,192]{1,0:T(8,128)S(1)}, u32[]{:S(2)}, u32[]{:S(2)}) collective-permute-start(f32[16,192]{1,0:T(8,128)S(1)} %add_add_fusion.1.refs_0_), channel_id=1, source_target_pairs={{0,16},{4,20},{8,24},{12,28},{16,0},{20,4},{24,8},{28,12},{1,17},{... | collective-permute-start | bytes 36872 | tf_op jit(solution)/shard_map/ppermute | solution.py:137
  20.4 10.8 %copy-start.6 = (f32[16,192]{1,0:T(8,128)}, f32[16,192]{1,0:T(8,128)S(1)}, u32[]{:S(2)}) copy-start(f32[16,192]{1,0:T(8,128)S(1)} %collective-permute-done.9.refs_7_) | copy-start | bytes 36868
  20.4 3.4 %collective-permute-start.5 = (f32[16,192]{1,0:T(8,128)S(1)}, f32[16,192]{1,0:T(8,128)S(1)}, u32[]{:S(2)}, u32[]{:S(2)}) collective-permute-start(f32[16,192]{1,0:T(8,128)S(1)} %add_add_fusion.1.refs_0_), channel_id=1, source_target_pairs={{0,12},{4,8},{8,4},{12,0},{16,28},{20,24},{24,20},{28,16},{1,13},{... | collective-permute-start | bytes 36872 | tf_op jit(solution)/shard_map/ppermute | solution.py:137
  21.1 10.1 %copy-start.1 = (s32[64,192]{1,0:T(8,128)}, s32[64,192]{1,0:T(8,128)S(1)}, u32[]{:S(2)}) copy-start(s32[64,192]{1,0:T(8,128)S(1)} %pad_add_fusion.refs_8_) | copy-start | bytes 147460
  21.1 10.1 %copy-start.7 = (f32[16,192]{1,0:T(8,128)}, f32[16,192]{1,0:T(8,128)S(1)}, u32[]{:S(2)}) copy-start(f32[16,192]{1,0:T(8,128)S(1)} %collective-permute-done.8.refs_6_) | copy-start | bytes 36868
  21.1 10.0 %collective-permute-start.12 = (s32[64,192]{1,0:T(8,128)S(1)}, s32[64,192]{1,0:T(8,128)S(1)}, u32[]{:S(2)}, u32[]{:S(2)}) collective-permute-start(s32[64,192]{1,0:T(8,128)S(1)} %pad_add_fusion.refs_8_), channel_id=1, source_target_pairs={{0,12},{4,8},{8,4},{12,0},{1,13},{5,9},{9,5},{13,1},{2,14},{6,10},... | collective-permute-start | bytes 147464 | tf_op jit(solution)/shard_map/ppermute | solution.py:127
  22.2 9.0 %copy-start.8 = (f32[16,192]{1,0:T(8,128)}, f32[16,192]{1,0:T(8,128)S(1)}, u32[]{:S(2)}) copy-start(f32[16,192]{1,0:T(8,128)S(1)} %collective-permute-done.7.refs_5_) | copy-start | bytes 36868
  22.2 8.9 %collective-permute-start.11 = (s32[64,192]{1,0:T(8,128)S(1)}, s32[64,192]{1,0:T(8,128)S(1)}, u32[]{:S(2)}, u32[]{:S(2)}) collective-permute-start(s32[64,192]{1,0:T(8,128)S(1)} %pad_add_fusion.refs_8_), channel_id=1, source_target_pairs={{0,8},{4,12},{8,0},{12,4},{1,9},{5,13},{9,1},{13,5},{2,10},{6,14},... | collective-permute-start | bytes 147464 | tf_op jit(solution)/shard_map/ppermute | solution.py:127
  23.7 7.5 %copy-start.9 = (f32[16,192]{1,0:T(8,128)}, f32[16,192]{1,0:T(8,128)S(1)}, u32[]{:S(2)}) copy-start(f32[16,192]{1,0:T(8,128)S(1)} %collective-permute-done.6.refs_4_) | copy-start | bytes 36868
  23.7 7.5 %collective-permute-start.10 = (s32[64,192]{1,0:T(8,128)S(1)}, s32[64,192]{1,0:T(8,128)S(1)}, u32[]{:S(2)}, u32[]{:S(2)}) collective-permute-start(s32[64,192]{1,0:T(8,128)S(1)} %pad_add_fusion.refs_8_), channel_id=1, source_target_pairs={{0,4},{4,0},{8,12},{12,8},{1,5},{5,1},{9,13},{13,9},{2,6},{6,2},{1... | collective-permute-start | bytes 147464 | tf_op jit(solution)/shard_map/ppermute | solution.py:127
  23.8 7.5 %copy-start.10 = (f32[16,192]{1,0:T(8,128)}, f32[16,192]{1,0:T(8,128)S(1)}, u32[]{:S(2)}) copy-start(f32[16,192]{1,0:T(8,128)S(1)} %collective-permute-done.5.refs_3_) | copy-start | bytes 36868
  23.8 7.4 %collective-permute-start.4 = (f32[16,192]{1,0:T(8,128)S(1)}, f32[16,192]{1,0:T(8,128)S(1)}, u32[]{:S(2)}, u32[]{:S(2)}) collective-permute-start(f32[16,192]{1,0:T(8,128)S(1)} %add_add_fusion.1.refs_0_), channel_id=1, source_target_pairs={{0,8},{4,12},{8,0},{12,4},{16,24},{20,28},{24,16},{28,20},{1,9},{5... | collective-permute-start | bytes 36872 | tf_op jit(solution)/shard_map/ppermute | solution.py:137
  25.2 0.7 %copy-start = (s32[16,4096]{1,0:T(8,128)}, s32[16,4096]{1,0:T(8,128)S(1)}, u32[]{:S(2)}) copy-start(s32[16,4096]{1,0:T(8,128)S(1)} %collective-permute-done.13.refs_1_) | copy-start | bytes 786436
  25.2 5.9 %collective-permute-start.3 = (f32[16,192]{1,0:T(8,128)S(1)}, f32[16,192]{1,0:T(8,128)S(1)}, u32[]{:S(2)}, u32[]{:S(2)}) collective-permute-start(f32[16,192]{1,0:T(8,128)S(1)} %add_add_fusion.1.refs_0_), channel_id=1, source_target_pairs={{0,4},{4,0},{8,12},{12,8},{16,20},{20,16},{24,28},{28,24},{1,5},{5... | collective-permute-start | bytes 36872 | tf_op jit(solution)/shard_map/ppermute | solution.py:137
  25.9 31.9 %copy-start.13 = (f32[32,128]{1,0:T(8,128)S(1)}, f32[32,128]{1,0:T(8,128)}, u32[]{:S(2)}) copy-start(f32[32,128]{1,0:T(8,128)} %param.11) | copy-start | bytes 49156
  31.1 0.6 %copy-start.11 = (f32[16,192]{1,0:T(8,128)}, f32[16,192]{1,0:T(8,128)S(1)}, u32[]{:S(2)}) copy-start(f32[16,192]{1,0:T(8,128)S(1)} %collective-permute-done.4.refs_2_) | copy-start | bytes 36868
  31.1 0.6 %copy-start.12 = (f32[16,192]{1,0:T(8,128)}, f32[16,192]{1,0:T(8,128)S(1)}, u32[]{:S(2)}) copy-start(f32[16,192]{1,0:T(8,128)S(1)} %collective-permute-done.3.refs_1_) | copy-start | bytes 36868
  31.2 0.6 %copy-start.3 = (s32[64,192]{1,0:T(8,128)}, s32[64,192]{1,0:T(8,128)S(1)}, u32[]{:S(2)}) copy-start(s32[64,192]{1,0:T(8,128)S(1)} %collective-permute-done.12.refs_11_) | copy-start | bytes 147460
  31.2 0.6 %copy-start.4 = (s32[64,192]{1,0:T(8,128)}, s32[64,192]{1,0:T(8,128)S(1)}, u32[]{:S(2)}) copy-start(s32[64,192]{1,0:T(8,128)S(1)} %collective-permute-done.11.refs_10_) | copy-start | bytes 147460
  31.8 0.6 %copy-start.5 = (s32[64,192]{1,0:T(8,128)}, s32[64,192]{1,0:T(8,128)S(1)}, u32[]{:S(2)}) copy-start(s32[64,192]{1,0:T(8,128)S(1)} %collective-permute-done.10.refs_9_) | copy-start | bytes 147460
  49.0 4.4 %collective-permute-start.14 = (f32[64,128]{1,0:T(8,128)}, f32[64,128]{1,0:T(8,128)S(1)}, u32[]{:S(2)}, u32[]{:S(2)}) collective-permute-start(f32[64,128]{1,0:T(8,128)} %get-tuple-element.9), channel_id=1, source_target_pairs={{0,1},{1,0},{2,3},{3,2},{4,5},{5,4},{6,7},{7,6},{8,9},{9,8},{10,11... | collective-permute-start | bytes 98312 | tf_op jit(solution)/shard_map/ppermute | solution.py:127
  49.0 5.1 %collective-permute-start.15 = (f32[64,128]{1,0:T(8,128)}, f32[64,128]{1,0:T(8,128)S(1)}, u32[]{:S(2)}, u32[]{:S(2)}) collective-permute-start(f32[64,128]{1,0:T(8,128)} %get-tuple-element.10), channel_id=1, source_target_pairs={{0,2},{1,3},{2,0},{3,1},{4,6},{5,7},{6,4},{7,5},{8,10},{9,11},{10,... | collective-permute-start | bytes 98312 | tf_op jit(solution)/shard_map/ppermute | solution.py:127
  51.1 5.9 %collective-permute-start.16 = (f32[64,128]{1,0:T(8,128)}, f32[64,128]{1,0:T(8,128)S(1)}, u32[]{:S(2)}, u32[]{:S(2)}) collective-permute-start(f32[64,128]{1,0:T(8,128)} %get-tuple-element.11), channel_id=1, source_target_pairs={{0,3},{1,2},{2,1},{3,0},{4,7},{5,6},{6,5},{7,4},{8,11},{9,10},{10,... | collective-permute-start | bytes 98312 | tf_op jit(solution)/shard_map/ppermute | solution.py:127
